TPU v7x, 256 devices: a whole 4x4x8 slice. The times are simulated.
256 devices in a mesh: row: 16 (over z, x_lo), col: 16 (over y, x_hi, core).
Axes of the slice: x: 4 (x_hi: 2, x_lo: 2; x = x_hi * 2 + x_lo), y: 4, z: 8, core: 2. Of those that a mesh axis runs over, the one named last changes fastest.
Arguments:
- resident_inverse: float32 [12288, 12288], P('row', 'col'), as said below
- factor_panel: float32 [2, 12288, 256], P(None, 'row', 'col'), may hold values from -0.109375 to 0.109375
- diag_inverse: float32 [2, 256, 256], P(None, 'row', 'col'), as said below
- ancestors: int32 [2, 48], replicated, may hold values from 0 to 1, as said below
- start_order: int32 [2], replicated, may hold values from 0 to 1, each once
Outputs:
- inverse_column: float32 [2, 12288, 256], P(None, 'row', 'col')
- inverse_row: float32 [2, 256, 12288], P(None, 'row', 'col')
- diagonal_block: float32 [2, 256, 256], P(None, 'row', 'col')
Inputs may be any that keep to these rules, and one draw needn't show every extreme that they name: `ancestors`: 1 marks a tile of 256 rows among the supernode's ancestor rows; each supernode marks between 32 and 48 tiles. `start_order`: a permutation of the supernodes. `resident_inverse`: symmetric. `diag_inverse`: each supernode's block is symmetric.
All inputs are finite; a program needn't handle non-finite values.
Results may differ from a plain program's by a relative error of at most 0.0001.
Values sent between devices are 32-bit elements; how exact they have to be, the bound alone decides.
A program may use at most 64 MiB of HBM per device.

v0:
```python
import jax
import jax.numpy as jnp
from jax import lax
from jax.sharding import PartitionSpec as P

TILE = 256


def in_order(pieces, dim):
    pieces = jnp.moveaxis(pieces, 0, dim)
    dims = pieces.shape
    return pieces.reshape(*dims[:dim], dims[dim] * dims[dim + 1], *dims[dim + 2 :])


def copy_for_each(value, axis):
    copies = jnp.broadcast_to(value, (lax.axis_size(axis), *value.shape))
    return lax.all_to_all(copies, axis, split_axis=0, concat_axis=0, tiled=True)


def collect(value, axis, dim):
    return in_order(copy_for_each(value, axis), dim)


def split_up(value, dim, size):
    dims = value.shape
    pieces = value.reshape(*dims[:dim], size, dims[dim] // size, *dims[dim + 1 :])
    return jnp.moveaxis(pieces, dim, 0)


def sent_and_summed(value, axis, dim):
    pieces = split_up(value, dim, lax.axis_size(axis))
    arrived = lax.all_to_all(pieces, axis, split_axis=0, concat_axis=0, tiled=True)
    return arrived.sum(axis=0)


def from_partner(block, axis, bit):
    count = lax.axis_size(axis)
    route = []
    for low in range(count):
        high = low | 1 << bit
        if high != low and high < count:
            route += [(low, high), (high, low)]
    return lax.ppermute(block, axis, route)


def on_device(resident_inverse, factor_panel, diag_inverse, ancestors, start_order):
    row_count = lax.axis_size("row")
    col_count = lax.axis_size("col")
    row_index = lax.axis_index("row")
    col_index = lax.axis_index("col")
    rows_here = resident_inverse.shape[0]
    cols_here = resident_inverse.shape[1]
    block_ratio = row_count // col_count
    listed = jnp.take(ancestors, start_order, axis=0)
    row_flags = jnp.repeat(listed, TILE, axis=1).astype(jnp.float32)
    row_masks = lax.dynamic_slice_in_dim(row_flags, row_index * rows_here, rows_here, 1)
    col_masks = lax.dynamic_slice_in_dim(row_flags, col_index * cols_here, cols_here, 1)
    sectioned_panel = jnp.take(factor_panel, start_order, axis=0)
    sectioned_diag = jnp.take(diag_inverse, start_order, axis=0)
    masked = sectioned_panel * row_masks[:, :, None]
    widened = collect(masked, "col", 2)
    row_terms = jnp.einsum(
        "sra,rc->sac",
        widened,
        resident_inverse,
        precision=lax.Precision.HIGHEST,
        preferred_element_type=jnp.float32,
    )
    row_summed = sent_and_summed(row_terms, "row", 1)
    row_result = -row_summed * col_masks[:, None, :]
    section_count = row_result.shape[0]
    narrow = row_result.shape[1]
    ratio_bits = block_ratio.bit_length() - 1
    col_bits = col_count.bit_length() - 1
    upper = row_index // block_ratio
    moving = row_result
    for bit_number in range(col_bits):
        across = from_partner(moving, "row", bit_number + ratio_bits)
        mirrored = from_partner(across, "col", bit_number)
        differs = upper // (1 << bit_number) % 2 != col_index // (1 << bit_number) % 2
        moving = jnp.where(differs, mirrored, moving)
    slots = jnp.swapaxes(moving.reshape(section_count, narrow, block_ratio, rows_here), 1, 2)
    col_result = jnp.swapaxes(slots.reshape(section_count, block_ratio * narrow, rows_here), 1, 2)
    diag_terms = jnp.einsum(
        "sra,srb->sab",
        widened,
        col_result,
        precision=lax.Precision.HIGHEST,
        preferred_element_type=jnp.float32,
    )
    diag_summed = sent_and_summed(diag_terms, "row", 1)
    return (col_result, row_result, sectioned_diag - diag_summed)


def solution(mesh):
    return jax.shard_map(
        on_device,
        mesh=mesh,
        in_specs=(P("row", "col"), P(None, "row", "col"), P(None, "row", "col"), P(), P()),
        out_specs=(P(None, "row", "col"), P(None, "row", "col"), P(None, "row", "col")),
        check_vma=False,
    )
```

profile of v0, /device:TPU:2, one launch (start us, length us, event | category | flops | bytes accessed | tf_op | source)
XLA Modules:
  0.0 148.3 jit_solution(12017470189973542292)
XLA Ops:
  0.7 0.8 compare_select_fusion
  1.5 0.7 compare_and_fusion
  2.1 1.4 gather_fusion
  3.6 0.6 gather_fusion.1
  4.7 29.5 %all_to_all.15 = f32[16,2,768,16]{2,3,1,0:T(8,128)S(1)} all-to-all(f32[16,2,768,16]{2,3,1,0:T(8,128)S(1)} %broadcast_in_dim.46), channel_id=1, replica_groups=mesh['row'=16,'col'=16] {'col'}, dimensions={0} | all-to-all | bytes 3145728 | tf_op jit(solution)/shard_map/all_to_all | solution.py:17
  34.2 4.0 %fusion.3 = f32[16,2,16,768]{3,2,0,1:T(8,128)S(1)} fusion(f32[768,768]{1,0:T(8,128)S(1)} %copy-done, f32[16,2,768,16]{2,3,1,0:T(8,128)S(1)} %all_to_all.15), kind=kOutput, calls=%fused_computation.6 | convolution fusion | flops 3623878656 | bytes 5505024 | tf_op jit(solution)/shard_map/sra,rc->sac/dot_general | solution.py:62
  38.4 47.4 %all_to_all.16 = f32[16,2,16,768]{3,2,1,0:T(8,128)} all-to-all(f32[16,2,16,768]{3,2,1,0:T(8,128)S(1)} %copy.12), channel_id=1, replica_groups=mesh['row'=16,'col'=16] {'row'}, dimensions={0} | all-to-all | bytes 3145728 | tf_op jit(solution)/shard_map/all_to_all | solution.py:32
  85.8 1.5 %reduce_sum.18 = f32[2,16,768]{2,1,0:T(8,128)S(1)} reduce(f32[16,2,16,768]{3,2,1,0:T(8,128)} %all_to_all.16, f32[]{:T(128)} %constant.167.clone.1), dimensions={0}, to_apply=%region_0.1 | reduce | flops 368640 | bytes 1671172 | tf_op jit(solution)/shard_map/reduce_sum | solution.py:33
  87.4 1.8 %collective-permute-start = (f32[2,16,768]{2,1,0:T(8,128)S(1)}, f32[2,16,768]{2,1,0:T(8,128)S(1)}, u32[]{:S(2)}, u32[]{:S(2)}) collective-permute-start(f32[2,16,768]{2,1,0:T(8,128)S(1)} %negate_multiply_fusion), channel_id=1, source_target_pairs={{0,16},{16,0},{32,48},{48,32},{64,80},{80,64},{96,112},{112,96},{1... | collective-permute-start | bytes 294920 | tf_op jit(solution)/shard_map/ppermute | solution.py:43
  89.2 2.9 %collective-permute-done = f32[2,16,768]{2,1,0:T(8,128)S(1)} collective-permute-done((f32[2,16,768]{2,1,0:T(8,128)S(1)}, f32[2,16,768]{2,1,0:T(8,128)S(1)}, u32[]{:S(2)}, u32[]{:S(2)}) %collective-permute-start) | collective-permute-done | bytes 98336 | tf_op jit(solution)/shard_map/ppermute | solution.py:43
  92.1 1.3 collective-permute-done.1
  93.8 4.6 %collective-permute-done.2 = f32[2,16,768]{2,1,0:T(8,128)S(1)} collective-permute-done((f32[2,16,768]{2,1,0:T(8,128)S(1)}, f32[2,16,768]{2,1,0:T(8,128)S(1)}, u32[]{:S(2)}, u32[]{:S(2)}) %collective-permute-start.2) | collective-permute-done | bytes 98336 | tf_op jit(solution)/shard_map/ppermute | solution.py:43
  98.3 2.3 %collective-permute-start.3 = (f32[2,16,768]{2,1,0:T(8,128)S(1)}, f32[2,16,768]{2,1,0:T(8,128)S(1)}, u32[]{:S(2)}, u32[]{:S(2)}) collective-permute-start(f32[2,16,768]{2,1,0:T(8,128)S(1)} %collective-permute-done.2), channel_id=1, source_target_pairs={{0,2},{2,0},{1,3},{3,1},{4,6},{6,4},{5,7},{7,5},{8,10},{10,8},{9,1... | collective-permute-start | bytes 294920 | tf_op jit(solution)/shard_map/ppermute | solution.py:43
  100.6 3.8 %collective-permute-done.3 = f32[2,16,768]{2,1,0:T(8,128)S(1)} collective-permute-done((f32[2,16,768]{2,1,0:T(8,128)S(1)}, f32[2,16,768]{2,1,0:T(8,128)S(1)}, u32[]{:S(2)}, u32[]{:S(2)}) %collective-permute-start.3) | collective-permute-done | bytes 98336 | tf_op jit(solution)/shard_map/ppermute | solution.py:43
  104.5 1.4 collective-permute-start.4
  105.8 5.0 %collective-permute-done.4 = f32[2,16,768]{2,1,0:T(8,128)S(1)} collective-permute-done((f32[2,16,768]{2,1,0:T(8,128)S(1)}, f32[2,16,768]{2,1,0:T(8,128)S(1)}, u32[]{:S(2)}, u32[]{:S(2)}) %collective-permute-start.4) | collective-permute-done | bytes 98336 | tf_op jit(solution)/shard_map/ppermute | solution.py:43
  110.8 0.8 collective-permute-start.5
  111.6 3.8 %collective-permute-done.5 = f32[2,16,768]{2,1,0:T(8,128)S(1)} collective-permute-done((f32[2,16,768]{2,1,0:T(8,128)S(1)}, f32[2,16,768]{2,1,0:T(8,128)S(1)}, u32[]{:S(2)}, u32[]{:S(2)}) %collective-permute-start.5) | collective-permute-done | bytes 98336 | tf_op jit(solution)/shard_map/ppermute | solution.py:43
  115.5 2.2 %collective-permute-start.6 = (f32[2,16,768]{2,1,0:T(8,128)S(1)}, f32[2,16,768]{2,1,0:T(8,128)S(1)}, u32[]{:S(2)}, u32[]{:S(2)}) collective-permute-start(f32[2,16,768]{2,1,0:T(8,128)S(1)} %broadcast_select_fusion.2), channel_id=1, source_target_pairs={{0,128},{128,0},{16,144},{144,16},{32,160},{160,32},{48,176},{176,... | collective-permute-start | bytes 294920 | tf_op jit(solution)/shard_map/ppermute | solution.py:43
  117.7 7.4 %collective-permute-done.6 = f32[2,16,768]{2,1,0:T(8,128)S(1)} collective-permute-done((f32[2,16,768]{2,1,0:T(8,128)S(1)}, f32[2,16,768]{2,1,0:T(8,128)S(1)}, u32[]{:S(2)}, u32[]{:S(2)}) %collective-permute-start.6) | collective-permute-done | bytes 98336 | tf_op jit(solution)/shard_map/ppermute | solution.py:43
  125.1 1.1 collective-permute-start.7
  126.3 0.5 gather_fusion.2
  126.9 1.5 %copy.11 = f32[16,2,768,16]{2,3,0,1:T(8,128)S(1)} copy(f32[16,2,768,16]{2,3,1,0:T(8,128)} %copy-done.1) | data formatting | bytes 3145728 | tf_op jit(solution)/shard_map/all_to_all | solution.py:17
  128.4 2.9 %collective-permute-done.7 = f32[2,16,768]{2,1,0:T(8,128)S(1)} collective-permute-done((f32[2,16,768]{2,1,0:T(8,128)S(1)}, f32[2,16,768]{2,1,0:T(8,128)S(1)}, u32[]{:S(2)}, u32[]{:S(2)}) %collective-permute-start.7) | collective-permute-done | bytes 98336 | tf_op jit(solution)/shard_map/ppermute | solution.py:43
  131.3 1.4 fusion.8
  132.9 0.7 reshape.53
  133.7 5.0 %all-to-all-start.2 = ((f32[16,1,512]{2,1,0:T(1,128)}), f32[16,1,512]{2,1,0:T(1,128)S(1)}, u32[]{:S(2)}, u32[]{:S(2)}) async-start(f32[16,1,512]{2,1,0:T(1,128)} %reshape.53), calls=%async_computation.2 | async-start | bytes 65536 | tf_op jit(solution)/shard_map/all_to_all | solution.py:32
  138.7 0.7 fusion.9
  139.3 6.8 %all-to-all-done.2 = f32[16,1,512]{2,1,0:T(1,128)S(1)} async-done(((f32[16,1,512]{2,1,0:T(1,128)}), f32[16,1,512]{2,1,0:T(1,128)S(1)}, u32[]{:S(2)}, u32[]{:S(2)}) %all-to-all-start.2) | async-done | bytes 32800 | tf_op jit(solution)/shard_map/all_to_all | solution.py:32
  146.2 0.5 broadcast.55
  146.7 0.7 reduce
  147.6 0.7 select_subtract_fusion
  (29 shorter events, 1.5 us)
Async XLA Ops:
  0.6 33.6 %copy-start = (f32[768,768]{1,0:T(8,128)S(1)}, f32[768,768]{1,0:T(8,128)}, u32[]{:S(2)}) copy-start(f32[768,768]{1,0:T(8,128)} %param.5) | copy-start | bytes 7077892
  0.6 3.0 %copy-start.3 = (s32[2,48]{1,0:T(2,128)S(1)}, s32[2,48]{1,0:T(2,128)}, u32[]{:S(2)}) copy-start(s32[2,48]{1,0:T(2,128)} %param.8) | copy-start | bytes 1156
  34.2 4.0 %copy-start.1 = (f32[16,2,768,16]{2,3,1,0:T(8,128)}, f32[16,2,768,16]{2,3,1,0:T(8,128)S(1)}, u32[]{:S(2)}) copy-start(f32[16,2,768,16]{2,3,1,0:T(8,128)S(1)} %all_to_all.15) | copy-start | bytes 4718596
  85.8 40.5 %copy-start.4 = (f32[2,16,16]{2,1,0:T(8,128)S(1)}, f32[2,16,16]{2,1,0:T(8,128)}, u32[]{:S(2)}) copy-start(f32[2,16,16]{2,1,0:T(8,128)} %param.7) | copy-start | bytes 6148
  87.3 41.1 %copy-start.2 = (f32[2,16,768]{2,1,0:T(8,128)}, f32[2,16,768]{2,1,0:T(8,128)S(1)}, u32[]{:S(2)}) copy-start(f32[2,16,768]{2,1,0:T(8,128)S(1)} %negate_multiply_fusion) | copy-start | bytes 294916
  87.4 4.7 %collective-permute-start = (f32[2,16,768]{2,1,0:T(8,128)S(1)}, f32[2,16,768]{2,1,0:T(8,128)S(1)}, u32[]{:S(2)}, u32[]{:S(2)}) collective-permute-start(f32[2,16,768]{2,1,0:T(8,128)S(1)} %negate_multiply_fusion), channel_id=1, source_target_pairs={{0,16},{16,0},{32,48},{48,32},{64,80},{80,64},{96,112},{112,96},{1... | collective-permute-start | bytes 294920 | tf_op jit(solution)/shard_map/ppermute | solution.py:43
  92.1 1.3 collective-permute-start.1
  93.4 4.9 %collective-permute-start.2 = (f32[2,16,768]{2,1,0:T(8,128)S(1)}, f32[2,16,768]{2,1,0:T(8,128)S(1)}, u32[]{:S(2)}, u32[]{:S(2)}) collective-permute-start(f32[2,16,768]{2,1,0:T(8,128)S(1)} %broadcast_select_fusion), channel_id=1, source_target_pairs={{0,32},{32,0},{16,48},{48,16},{64,96},{96,64},{80,112},{112,80},{1... | collective-permute-start | bytes 294920 | tf_op jit(solution)/shard_map/ppermute | solution.py:43
  98.3 6.1 %collective-permute-start.3 = (f32[2,16,768]{2,1,0:T(8,128)S(1)}, f32[2,16,768]{2,1,0:T(8,128)S(1)}, u32[]{:S(2)}, u32[]{:S(2)}) collective-permute-start(f32[2,16,768]{2,1,0:T(8,128)S(1)} %collective-permute-done.2), channel_id=1, source_target_pairs={{0,2},{2,0},{1,3},{3,1},{4,6},{6,4},{5,7},{7,5},{8,10},{10,8},{9,1... | collective-permute-start | bytes 294920 | tf_op jit(solution)/shard_map/ppermute | solution.py:43
  104.5 6.4 %collective-permute-start.4 = (f32[2,16,768]{2,1,0:T(8,128)S(1)}, f32[2,16,768]{2,1,0:T(8,128)S(1)}, u32[]{:S(2)}, u32[]{:S(2)}) collective-permute-start(f32[2,16,768]{2,1,0:T(8,128)S(1)} %broadcast_select_fusion.1), channel_id=1, source_target_pairs={{0,64},{64,0},{16,80},{80,16},{32,96},{96,32},{48,112},{112,48},{1... | collective-permute-start | bytes 294920 | tf_op jit(solution)/shard_map/ppermute | solution.py:43
  110.8 4.6 %collective-permute-start.5 = (f32[2,16,768]{2,1,0:T(8,128)S(1)}, f32[2,16,768]{2,1,0:T(8,128)S(1)}, u32[]{:S(2)}, u32[]{:S(2)}) collective-permute-start(f32[2,16,768]{2,1,0:T(8,128)S(1)} %collective-permute-done.4), channel_id=1, source_target_pairs={{0,4},{4,0},{1,5},{5,1},{2,6},{6,2},{3,7},{7,3},{8,12},{12,8},{9,1... | collective-permute-start | bytes 294920 | tf_op jit(solution)/shard_map/ppermute | solution.py:43
  115.5 9.7 %collective-permute-start.6 = (f32[2,16,768]{2,1,0:T(8,128)S(1)}, f32[2,16,768]{2,1,0:T(8,128)S(1)}, u32[]{:S(2)}, u32[]{:S(2)}) collective-permute-start(f32[2,16,768]{2,1,0:T(8,128)S(1)} %broadcast_select_fusion.2), channel_id=1, source_target_pairs={{0,128},{128,0},{16,144},{144,16},{32,160},{160,32},{48,176},{176,... | collective-permute-start | bytes 294920 | tf_op jit(solution)/shard_map/ppermute | solution.py:43
  125.1 6.1 %collective-permute-start.7 = (f32[2,16,768]{2,1,0:T(8,128)S(1)}, f32[2,16,768]{2,1,0:T(8,128)S(1)}, u32[]{:S(2)}, u32[]{:S(2)}) collective-permute-start(f32[2,16,768]{2,1,0:T(8,128)S(1)} %collective-permute-done.6), channel_id=1, source_target_pairs={{0,8},{8,0},{1,9},{9,1},{2,10},{10,2},{3,11},{11,3},{4,12},{12,4},... | collective-permute-start | bytes 294920 | tf_op jit(solution)/shard_map/ppermute | solution.py:43
  133.7 12.5 %all-to-all-start.2 = ((f32[16,1,512]{2,1,0:T(1,128)}), f32[16,1,512]{2,1,0:T(1,128)S(1)}, u32[]{:S(2)}, u32[]{:S(2)}) async-start(f32[16,1,512]{2,1,0:T(1,128)} %reshape.53), calls=%async_computation.2 | async-start | bytes 65536 | tf_op jit(solution)/shard_map/all_to_all | solution.py:32
where the time goes:
time: 149 us; the launch traced here: 148 us
  blocking collectives  77 us (52%)
  waiting for transfers between devices  38.5 us (26%)
  starting transfers between devices  15.1 us (10%)
  local copies, waits for them, and re-layouts  6.22 us (4%)
  matrix products  5.46 us (4%)
  other arithmetic  5.27 us (4%)
    all_to_all x1, blocking collectives, sent_and_summed(): lax.all_to_all(pieces, axis, split_axis=0, concat_axis=0, tiled=True)  47.4 us
    ppermute x8, waiting for transfers between devices, from_partner(): return lax.ppermute(block, axis, route)  31.7 us
    all_to_all x1, blocking collectives, copy_for_each(): return lax.all_to_all(copies, axis, split_axis=0, concat_axis=0, tiled=True)  29.5 us
    ppermute x8, starting transfers between devices, from_partner(): return lax.ppermute(block, axis, route)  10.1 us
    all_to_all x1, waiting for transfers between devices, sent_and_summed(): lax.all_to_all(pieces, axis, split_axis=0, concat_axis=0, tiled=True)  6.83 us
    all_to_all x1, starting transfers between devices, sent_and_summed(): lax.all_to_all(pieces, axis, split_axis=0, concat_axis=0, tiled=True)  4.99 us
    dot_general x1, matrix products, on_device(): jnp.einsum('sra,rc->sac', widened, resident_inverse, precision=lax.Precis...  4.03 us
  transfers between devices with their start and end apart: 9, of which 9 were waited for; matrix products, arithmetic and copies ran while one was open for 2% of the time, Pallas kernels for 0%

commit v1 on v0

v1 whole, which is shorter than its diff:
```python
import jax
import jax.numpy as jnp
from jax import lax
from jax.experimental import pallas as pl
from jax.experimental.pallas import tpu as pltpu
from jax.sharding import PartitionSpec as P

MESH = pl.DeviceIdType.MESH
TILE = 256
S = 2
NR = 16
NC = 16
NZ = 8
NY = 4
ROWS = 768
COLS = 768
N = 16
W = 256
CHIPS = [(dy, dx) for dy in (0, 1, 3, 2) for dx in (0, 1) if (dy, dx) != (0, 0)]
BF = jnp.bfloat16
F32 = jnp.float32


def split(x):
    hi = x.astype(BF)
    lo = (x - hi.astype(F32)).astype(BF)
    return hi, lo


def chain_length(s, d):
    return NZ // 2 if (s == 0) == (d == 1) else NZ // 2 - 1


def kernel(
    anc, order, a_hbm, p_ref, dinv_ref,
    row_ref, col_ref, diag_ref,
    a_buf, a_hi, a_lo, mine, pt, t, rp, f, xr, m, mpad, dp, dr,
    a_sem, ag_send, ag_recv, sib_send, sib_recv, fw_send, fw_recv,
    rs_send, rs_recv, x_send, x_recv, m_send, m_recv, d_send, d_recv,
):
    r = lax.axis_index("row")
    c = lax.axis_index("col")
    z, xl = r // 2, r % 2
    y, xh, k = c // 4, (c // 2) % 2, c % 2
    off_diagonal = r != c

    def col_at(dy, dx, core):
        return ((y + dy) % NY) * 4 + ((xh + dx) % 2) * 2 + core

    def row_at(dz, dx):
        return ((z + dz) % NZ) * 2 + (xl + dx) % 2

    sibling = (r, col_at(0, 0, 1 - k))
    x_peer = (row_at(0, 1), c)
    row_peers = [(j // 2, j % 2) for j in range(1, NR)]

    a_copy = pltpu.make_async_copy(a_hbm, a_buf, a_sem)
    a_copy.start()

    barrier = pltpu.get_barrier_semaphore()

    def greet(device):
        pl.semaphore_signal(barrier, inc=1, device_id=device, device_id_type=MESH)

    greet(sibling)
    for dy, dx in CHIPS:
        greet((r, col_at(dy, dx, k)))
    for dz, dx in row_peers:
        greet((row_at(dz, dx), c))

    @pl.when(off_diagonal)
    def _():
        greet((c, r))

    def flag(s, tile):
        return anc[order[s], tile].astype(F32)

    first = order[0] == 0
    for s in range(S):
        chosen = jnp.where(first, p_ref[s], p_ref[1 - s])
        for b in range(ROWS // TILE):
            here = pl.ds(b * TILE, TILE)
            mine[s, :, here] = chosen[:, b * TILE : (b + 1) * TILE] * flag(s, r * 3 + b)

    pl.semaphore_wait(barrier, 1 + len(CHIPS) + len(row_peers) + off_diagonal.astype(jnp.int32))

    def remote(src, dst, send, recv, device):
        return pltpu.make_async_remote_copy(
            src_ref=src, dst_ref=dst, send_sem=send, recv_sem=recv, device_id=device, device_id_type=MESH
        )

    sent = []
    for s in range(S):
        for i, (dy, dx) in enumerate(CHIPS):
            copy = remote(mine.at[s], pt.at[s, c], ag_send.at[s, i], ag_recv.at[s, i], (r, col_at(dy, dx, k)))
            copy.start()
            sent.append(copy)
        copy = remote(mine.at[s], pt.at[s, c], sib_send.at[s], sib_recv.at[s], sibling)
        copy.start()
        sent.append(copy)
        pt[s, c] = mine[s]

    a_copy.wait()
    for b in range(3):
        here = pl.ds(b * TILE, TILE)
        hi, lo = split(a_buf[here, :])
        a_hi[here, :] = hi
        a_lo[here, :] = lo

    def gathered(s):
        for i, (dy, dx) in enumerate(CHIPS):
            slot = col_at(-dy, dx, k)
            remote(mine.at[s], pt.at[s, slot], ag_send.at[s, i], ag_recv.at[s, i], sibling).wait_recv()
            copy = remote(pt.at[s, slot], pt.at[s, slot], fw_send.at[s, i], fw_recv.at[s, i], sibling)
            copy.start()
            sent.append(copy)
        other = col_at(0, 0, 1 - k)
        remote(mine.at[s], pt.at[s, other], sib_send.at[s], sib_recv.at[s], sibling).wait_recv()
        for i, (dy, dx) in enumerate(CHIPS):
            slot = col_at(-dy, dx, 1 - k)
            remote(mine.at[s], pt.at[s, slot], fw_send.at[s, i], fw_recv.at[s, i], sibling).wait_recv()

    def multiply(s):
        hi, lo = split(pt[s].reshape(W, ROWS))

        for b in range(3):
            here = pl.ds(b * TILE, TILE)
            u, v = a_hi[:, here], a_lo[:, here]
            total = jnp.dot(hi, u, preferred_element_type=F32)
            total += jnp.dot(hi, v, preferred_element_type=F32)
            total += jnp.dot(lo, u, preferred_element_type=F32)
            t[s, :, :, here] = total.reshape(NZ, 32, TILE)

    def hop(s, d, j):
        length = chain_length(s, d)
        e = 0 if d == 1 else 1
        target = (z + d * (length - j)) % NZ
        if j == 0:
            src = t.at[s, target]
        else:
            arrived(s, d, j - 1)
            src = rp.at[s, e, j - 1]
            src[...] += t[s, target]
        copy = remote(src, rp.at[s, e, j], rs_send.at[s, e, j], rs_recv.at[s, e, j], (row_at(d, 0), c))
        copy.start()
        sent.append(copy)

    def arrived(s, d, j):
        e = 0 if d == 1 else 1
        remote(t.at[s, 0], rp.at[s, e, j], rs_send.at[s, e, j], rs_recv.at[s, e, j], x_peer).wait_recv()

    for s in range(S):
        gathered(s)
        multiply(s)
        for d in (1, -1):
            hop(s, d, 0)
    for j in range(1, NZ // 2):
        for s in range(S):
            for d in (1, -1):
                if j < chain_length(s, d):
                    hop(s, d, j)

    for s in range(S):
        ends = [chain_length(s, d) - 1 for d in (1, -1)]
        arrived(s, 1, ends[0])
        arrived(s, -1, ends[1])
        f[s] = (t[s, z] + rp[s, 0, ends[0]] + rp[s, 1, ends[1]]).reshape(2, N, COLS)
        copy = remote(f.at[s, 1 - xl], xr.at[s], x_send.at[s], x_recv.at[s], x_peer)
        copy.start()
        sent.append(copy)

    mpad[...] = jnp.zeros_like(mpad)
    for s in range(S):
        remote(f.at[s, 0], xr.at[s], x_send.at[s], x_recv.at[s], x_peer).wait_recv()
        for b in range(COLS // TILE):
            here = pl.ds(b * TILE, TILE)
            row_ref[s, :, here] = (f[s, xl, :, here] + xr[s, :, here]) * -flag(s, c * 3 + b)

        @pl.when(off_diagonal)
        def _(s=s):
            remote(row_ref.at[s], m.at[s], m_send.at[s], m_recv.at[s], (c, r)).start()

        @pl.when(jnp.logical_not(off_diagonal))
        def _(s=s):
            m[s] = row_ref[s]

    total = jnp.zeros((W, 128), F32)
    for s in range(S):

        @pl.when(off_diagonal)
        def _(s=s):
            remote(row_ref.at[s], m.at[s], m_send.at[s], m_recv.at[s], (c, r)).wait_recv()

        col_ref[s] = m[s]
        mpad[s, pl.ds(s * N, N), :] = m[s]
        hi, lo = split(pt[s].reshape(W, ROWS))
        u, v = split(mpad[s])
        for left, right in ((hi, u), (hi, v), (lo, u)):
            total += lax.dot_general(left, right, (((1,), (1,)), ((), ())), preferred_element_type=F32)
    halves = total.reshape(NR, 2, 8, 128)
    dp[...] = halves[:, 0] + pltpu.roll(halves[:, 1].reshape(NR * 8, 128), 32, 1).reshape(NR, 8, 128)
    for i, (dz, dx) in enumerate(row_peers):
        to = row_at(dz, dx)
        copy = remote(dp.at[to], dr.at[i], d_send.at[i], d_recv.at[i], (to, c))
        copy.start()
        sent.append(copy)
    summed = dp[r]
    for i in range(NR - 1):
        remote(dp.at[0], dr.at[i], d_send.at[i], d_recv.at[i], x_peer).wait_recv()
        summed += dr[i]
    for s in range(S):
        chosen = jnp.where(first, dinv_ref[s], dinv_ref[1 - s])
        for h in range(2):
            at = h * 32 + s * N
            diag_ref[s, pl.ds(h * 8, 8), :] = chosen[h * 8 : h * 8 + 8] - summed[:, at : at + N]

    for copy in sent:
        copy.wait_send()
    for s in range(S):

        @pl.when(off_diagonal)
        def _(s=s):
            remote(row_ref.at[s], m.at[s], m_send.at[s], m_recv.at[s], (c, r)).wait_send()


def on_device(resident_inverse, factor_panel, diag_inverse, ancestors, start_order):
    vmem = pl.BlockSpec(memory_space=pltpu.VMEM)
    smem = pl.BlockSpec(memory_space=pltpu.SMEM)
    dma = pltpu.SemaphoreType.DMA
    half = NZ // 2
    chips = len(CHIPS)
    row, col, diag = pl.pallas_call(
        kernel,
        out_shape=(
            jax.ShapeDtypeStruct((S, N, COLS), F32),
            jax.ShapeDtypeStruct((S, N, ROWS), F32),
            jax.ShapeDtypeStruct((S, N, N), F32),
        ),
        in_specs=[smem, smem, pl.BlockSpec(memory_space=pl.ANY), vmem, vmem],
        out_specs=(vmem, vmem, vmem),
        scratch_shapes=[
            pltpu.VMEM((ROWS, COLS), F32),
            pltpu.VMEM((ROWS, COLS), BF),
            pltpu.VMEM((ROWS, COLS), BF),
            pltpu.VMEM((S, N, ROWS), F32),
            pltpu.VMEM((S, NC, N, ROWS), F32),
            pltpu.VMEM((S, NZ, 2 * N, COLS), F32),
            pltpu.VMEM((S, 2, half, 2 * N, COLS), F32),
            pltpu.VMEM((S, 2, N, COLS), F32),
            pltpu.VMEM((S, N, COLS), F32),
            pltpu.VMEM((S, N, ROWS), F32),
            pltpu.VMEM((S, 128, ROWS), F32),
            pltpu.VMEM((NR, 8, 128), F32),
            pltpu.VMEM((NR - 1, 8, 128), F32),
            dma,
            dma((S, chips)),
            dma((S, chips)),
            dma((S,)),
            dma((S,)),
            dma((S, chips)),
            dma((S, chips)),
            dma((S, 2, half)),
            dma((S, 2, half)),
            dma((S,)),
            dma((S,)),
            dma((S,)),
            dma((S,)),
            dma((NR - 1,)),
            dma((NR - 1,)),
        ],
        compiler_params=pltpu.CompilerParams(
            collective_id=0, has_side_effects=True, vmem_limit_bytes=48 * 1024 * 1024
        ),
        name="selected_inverse",
    )(ancestors, start_order, resident_inverse, jnp.swapaxes(factor_panel, 1, 2), diag_inverse)
    return jnp.swapaxes(col, 1, 2), row, diag


def solution(mesh):
    return jax.shard_map(
        on_device,
        mesh=mesh,
        in_specs=(P("row", "col"), P(None, "row", "col"), P(None, "row", "col"), P(), P()),
        out_specs=(P(None, "row", "col"), P(None, "row", "col"), P(None, "row", "col")),
        check_vma=False,
    )
```

time: 149 us -> 69.8 us (0.47)
  blocking collectives: 77 us -> 0 us
  Pallas kernels: 0 us -> 62.5 us
  waiting for transfers between devices: 38.5 us -> 0 us
  starting transfers between devices: 15.1 us -> 0 us
  matrix products: 5.46 us -> 0 us
  other arithmetic: 5.27 us -> 0 us
    all_to_all x2 -> x0, blocking collectives: 77 us -> none  [the longest x1 47.4 us: sent_and_summed(): lax.all_to_all(pieces, axis, split_axis=0, concat_axis=0, tiled=True)]
    pallas_call x0 -> x1, Pallas kernels: none -> 62.5 us  [on_device(): pl.pallas_call(kernel, out_shape=(jax.ShapeDtypeStruct((S, N, COLS), F32)...]
    ppermute x8 -> x0, waiting for transfers between devices: 31.7 us -> none  [from_partner(): return lax.ppermute(block, axis, route)]
    ppermute x8 -> x0, starting transfers between devices: 10.1 us -> none  [from_partner(): return lax.ppermute(block, axis, route)]
    all_to_all x1 -> x0, waiting for transfers between devices: 6.83 us -> none  [sent_and_summed(): lax.all_to_all(pieces, axis, split_axis=0, concat_axis=0, tiled=True)]
    dot_general x2 -> x0, matrix products: 5.46 us -> none  [the longest x1 4.03 us: on_device(): jnp.einsum('sra,rc->sac', widened, resident_inverse, precision=lax.Precis...]
    unnamed x14 -> x13, local copies, waits for them, and re-layouts: 1.05 us -> 6.49 us
    all_to_all x1 -> x0, starting transfers between devices: 4.99 us -> none  [sent_and_summed(): lax.all_to_all(pieces, axis, split_axis=0, concat_axis=0, tiled=True)]
  transfers between devices with their start and end apart: 9 -> 0, of which waited for: 9 -> 0; matrix products, arithmetic and copies ran while one was open for 2% -> 0% of each run, Pallas kernels for 0% -> 0%
where the time goes in v1:
time: 69.8 us; the launch traced here: 69.6 us
  Pallas kernels  62.5 us (90%)
  local copies, waits for them, and re-layouts  6.49 us (9%)
    pallas_call x1, Pallas kernels, on_device(): pl.pallas_call(kernel, out_shape=(jax.ShapeDtypeStruct((S, N, COLS), F32)...  62.5 us
    unnamed x13, local copies, waits for them, and re-layouts  6.49 us

profile of v1, /device:TPU:2, one launch (start us, length us, event | category | flops | bytes accessed | tf_op | source)
XLA Modules:
  0.0 69.6 jit_solution(8874384417017458218)
XLA Ops:
  0.6 0.0 copy-start
  0.6 1.7 %copy-done = f32[768,768]{1,0:T(8,128)S(1)} copy-done((f32[768,768]{1,0:T(8,128)S(1)}, f32[768,768]{1,0:T(8,128)}, u32[]{:S(2)}) %copy-start) | copy-done | bytes 2359320
  2.3 0.0 copy-start.1
  2.3 0.9 %copy-done.1 = f32[2,768,16]{1,2,0:T(8,128)S(1)} copy-done((f32[2,768,16]{1,2,0:T(8,128)S(1)}, f32[2,768,16]{1,2,0:T(8,128)}, u32[]{:S(2)}) %copy-start.1) | copy-done | bytes 98328
  3.2 0.0 copy-start.2
  3.2 0.7 %copy-done.2 = f32[2,16,16]{2,1,0:T(8,128)S(1)} copy-done((f32[2,16,16]{2,1,0:T(8,128)S(1)}, f32[2,16,16]{2,1,0:T(8,128)}, u32[]{:S(2)}) %copy-start.2) | copy-done | bytes 2072
  3.9 0.0 copy-start.3
  3.9 0.7 copy-done.3
  4.6 0.0 copy-start.4
  4.6 0.7 copy-done.4
  5.2 62.5 %selected_inverse.1 = (f32[2,16,768]{2,1,0:T(8,128)S(1)}, f32[2,16,768]{2,1,0:T(8,128)S(1)}, f32[2,16,16]{2,1,0:T(8,128)S(1)}) custom-call(s32[2,48]{1,0:T(2,128)S(1)} %copy-done.3, s32[2]{0:T(128)S(1)} %copy-done.4, f32[768,768]{1,0:T(8,128)S(1)} %copy-done, f32[2,16,768]{2,1,0:T(8,128)S(1)} %bitcast.2, f32[2,16,16]{2,1,0:T(8,128)S(1)} %copy-done.2), custom_call_target="tpu_custom_call" | custom-call | tf_op jit(solution)/shard_map/selected_inverse/pallas_call | solution.py:232
  67.7 0.6 copy.11
  68.3 0.6 copy.12
  69.0 0.6 copy.13
Async XLA Ops:
  0.6 1.7 %copy-start = (f32[768,768]{1,0:T(8,128)S(1)}, f32[768,768]{1,0:T(8,128)}, u32[]{:S(2)}) copy-start(f32[768,768]{1,0:T(8,128)} %a_hbm.1) | copy-start | bytes 7077892
  2.3 0.9 %copy-start.1 = (f32[2,768,16]{1,2,0:T(8,128)S(1)}, f32[2,768,16]{1,2,0:T(8,128)}, u32[]{:S(2)}) copy-start(f32[2,768,16]{1,2,0:T(8,128)} %param.6) | copy-start | bytes 294916
  3.2 0.7 %copy-start.2 = (f32[2,16,16]{2,1,0:T(8,128)S(1)}, f32[2,16,16]{2,1,0:T(8,128)}, u32[]{:S(2)}) copy-start(f32[2,16,16]{2,1,0:T(8,128)} %dinv_ref.1) | copy-start | bytes 6148
  3.9 0.7 copy-start.3
  4.6 0.7 copy-start.4

commit v2 on v0

v2 whole, which is shorter than its diff:
```python
import jax
import jax.numpy as jnp
from jax import lax
from jax.experimental import pallas as pl
from jax.experimental.pallas import tpu as pltpu
from jax.sharding import PartitionSpec as P

MESH = pl.DeviceIdType.MESH
BF = jnp.bfloat16
F32 = jnp.float32
TILE = 256
S = 2
U = 4
NR = 16
NC = 16
NZ = 8
NY = 4
ROWS = 768
COLS = 768
TILES = ROWS // TILE
N = 16
H = 8
W = NC * H
CHIPS = [(2, 1), (1, 1), (3, 1), (2, 0), (0, 1), (1, 0), (3, 0)]
CHAINS = [(1, 0), (-1, 1), (-1, 0), (1, 1)]
ROW_PEERS = sorted(((j // 2, j % 2) for j in range(1, NR)), key=lambda p: -min(p[0], NZ - p[0]) - p[1])


def split(x):
    hi = x.astype(BF)
    lo = (x - hi.astype(F32)).astype(BF)
    return hi, lo


def hops(d, g):
    return NZ // 2 if (d == 1) == (g == 0) else NZ // 2 - 1


def kernel(
    order_hbm, anc_hbm, a_hbm, p_hbm, dinv_hbm,
    row_ref, col_ref, diag_ref,
    order, anc, a_buf, a_hi, a_lo, dinv, pt, p_hi, p_lo, t, rp, fin, xr, rows, m, dp, dr,
    local_sem, ag_send, ag_recv, sib_send, sib_recv, fw_send, fw_recv,
    rs_send, rs_recv, fin_recv, x_send, x_recv, m_send, m_recv, d_send, d_recv,
):
    r = lax.axis_index("row")
    c = lax.axis_index("col")
    z, xl = r // 2, r % 2
    y, xh, k = c // 4, (c // 2) % 2, c % 2
    off_diagonal = r != c

    def col_at(dy, dx, core):
        return ((y + dy) % NY) * 4 + ((xh + dx) % 2) * 2 + core

    def row_at(dz, dx):
        return ((z + dz) % NZ) * 2 + (xl + dx) % 2

    sibling = (r, col_at(0, 0, 1 - k))
    x_peer = (row_at(0, 1), c)
    barrier = pltpu.get_barrier_semaphore()
    greeted = [(r, col_at(dy, dx, k)) for dy, dx in CHIPS]
    greeted += [(row_at(1, 0), c), (row_at(-1, 0), c), (row_at(1, 1), c), (row_at(-1, 1), c), x_peer, sibling]
    for device in greeted:
        pl.semaphore_signal(barrier, inc=1, device_id=device, device_id_type=MESH)

    locals_ = [
        pltpu.make_async_copy(a_hbm, a_buf, local_sem.at[0]),
        pltpu.make_async_copy(anc_hbm, anc, local_sem.at[1]),
        pltpu.make_async_copy(order_hbm, order, local_sem.at[2]),
        pltpu.make_async_copy(dinv_hbm, dinv, local_sem.at[3]),
    ]
    for u in range(U):
        mine = p_hbm.at[u // 2, pl.ds(u % 2 * H, H)]
        locals_.append(pltpu.make_async_copy(mine, pt.at[u, c], local_sem.at[4 + u]))
    for copy in locals_:
        copy.start()
    pl.semaphore_wait(barrier, len(greeted))

    sent = []

    def remote(src, dst, send, recv, device):
        return pltpu.make_async_remote_copy(
            src_ref=src, dst_ref=dst, send_sem=send, recv_sem=recv, device_id=device, device_id_type=MESH
        )

    def send(*args):
        copy = remote(*args)
        copy.start()
        sent.append(copy)

    def spread(u):
        mine = p_hbm.at[u // 2, pl.ds(u % 2 * H, H)]
        for i, (dy, dx) in enumerate(CHIPS):
            send(mine, pt.at[u, c], ag_send.at[u, i], ag_recv.at[u, i], (r, col_at(dy, dx, k)))
        send(mine, pt.at[u, c], sib_send.at[u], sib_recv.at[u], sibling)

    def forward(u):
        for i, (dy, dx) in list(enumerate(CHIPS))[::-1]:
            slot = col_at(-dy, dx, k)
            remote(pt.at[u, slot], pt.at[u, slot], ag_send.at[u, i], ag_recv.at[u, i], sibling).wait_recv()
            send(pt.at[u, slot], pt.at[u, slot], fw_send.at[u, i], fw_recv.at[u, i], sibling)

    def multiply(u):
        locals_[4 + u].wait()
        other = col_at(0, 0, 1 - k)
        remote(pt.at[u, other], pt.at[u, other], sib_send.at[u], sib_recv.at[u], sibling).wait_recv()
        for i, (dy, dx) in enumerate(CHIPS):
            slot = col_at(-dy, dx, 1 - k)
            remote(pt.at[u, slot], pt.at[u, slot], fw_send.at[u, i], fw_recv.at[u, i], sibling).wait_recv()
        for b in range(TILES):
            here = pl.ds(b * TILE, TILE)
            flag = anc[u // 2, r * TILES + b].astype(F32)
            hi, lo = split(pt[u, :, :, here].reshape(W, TILE) * flag)
            p_hi[u, :, here] = hi
            p_lo[u, :, here] = lo
        for b in range(TILES):
            here = pl.ds(b * TILE, TILE)
            v, w = a_hi[:, here], a_lo[:, here]
            total = jnp.dot(p_hi[u], v, preferred_element_type=F32)
            total += jnp.dot(p_hi[u], w, preferred_element_type=F32)
            total += jnp.dot(p_lo[u], v, preferred_element_type=F32)
            t[u, :, :, :, here] = total.reshape(NZ, 2, H, TILE)

    def side(d):
        return 0 if d == 1 else 1

    def hop(u, j):
        for d, g in CHAINS:
            last = hops(d, g) - 1
            if j > last:
                continue
            e = side(d)
            block = t.at[u, (z + d * (last + 1 - j)) % NZ, (xl + g) % 2]
            if j == 0:
                src = block
            else:
                src = rp.at[u, e, g, j - 1]
                remote(src, src, rs_send.at[u, e, g, j - 1], rs_recv.at[u, e, g, j - 1], x_peer).wait_recv()
                src[...] += block[...]
            if j == last:
                send(src, fin.at[u, e, g], rs_send.at[u, e, g, j], fin_recv.at[u, e, g], (row_at(d, g), c))
            else:
                send(src, rp.at[u, e, g, j], rs_send.at[u, e, g, j], rs_recv.at[u, e, g, j], (row_at(d, 0), c))
        if j == 0:
            send(t.at[u, z, 1 - xl], xr.at[u], x_send.at[u], x_recv.at[u], x_peer)

    def mirror(u):
        there = m.at[u // 2, pl.ds(u % 2 * H, H)]
        return remote(rows.at[u], there, m_send.at[u], m_recv.at[u], (c, r))

    def finish(u):
        remote(xr.at[u], xr.at[u], x_send.at[u], x_recv.at[u], x_peer).wait_recv()
        for d, g in CHAINS[2:] + CHAINS[:2]:
            e = side(d)
            there = fin.at[u, e, g]
            remote(there, there, rs_send.at[u, e, g, 0], fin_recv.at[u, e, g], x_peer).wait_recv()
        for b in range(TILES):
            here = pl.ds(b * TILE, TILE)
            total = t[u, z, xl, :, here] + xr[u, :, here]
            total += fin[u, 0, 0, :, here] + fin[u, 0, 1, :, here]
            total += fin[u, 1, 0, :, here] + fin[u, 1, 1, :, here]
            rows[u, :, here] = total * -anc[u // 2, c * TILES + b].astype(F32)

        @pl.when(off_diagonal)
        def _():
            mirror(u).start()

        @pl.when(jnp.logical_not(off_diagonal))
        def _():
            m[u // 2, pl.ds(u % 2 * H, H), :] = rows[u]

    def diagonal(s):
        for h in range(2):

            @pl.when(off_diagonal)
            def _():
                mirror(2 * s + h).wait_recv()

        v, w = split(m[s])
        halves = []
        for h in range(2):
            total = jnp.zeros((W, 128), F32)
            for left, right in ((p_hi, v), (p_hi, w), (p_lo, v)):
                total += lax.dot_general(
                    left[2 * s + h], right, (((1,), (1,)), ((), ())), preferred_element_type=F32
                )
            halves.append(total)
        dp[s] = (halves[0] + pltpu.roll(halves[1], N, 1)).reshape(NR, 8, 128)
        for i, (dz, dx) in enumerate(ROW_PEERS):
            to = row_at(dz, dx)
            send(dp.at[s, to], dr.at[s, i], d_send.at[s, i], d_recv.at[s, i], (to, c))

    def add_diagonal(s):
        total = dp[s, r]
        for i in list(range(NR - 1))[::-1]:
            remote(dr.at[s, i], dr.at[s, i], d_send.at[s, i], d_recv.at[s, i], x_peer).wait_recv()
            total += dr[s, i]
        return total

    spread(0)
    m[:, pl.ds(N, 128 - N), :] = jnp.zeros((S, 128 - N, ROWS), F32)
    locals_[0].wait()
    for b in range(TILES):
        here = pl.ds(b * TILE, TILE)
        hi, lo = split(a_buf[here, :])
        a_hi[here, :] = hi
        a_lo[here, :] = lo
    locals_[1].wait()
    spread(1)
    forward(0)
    spread(2)
    multiply(0)
    hop(0, 0)
    forward(1)
    spread(3)
    multiply(1)
    hop(1, 0)
    hop(0, 1)
    forward(2)
    multiply(2)
    hop(2, 0)
    hop(1, 1)
    hop(0, 2)
    forward(3)
    multiply(3)
    hop(3, 0)
    hop(2, 1)
    hop(1, 2)
    hop(0, 3)
    hop(3, 1)
    hop(2, 2)
    hop(1, 3)
    finish(0)
    hop(3, 2)
    hop(2, 3)
    finish(1)
    hop(3, 3)
    finish(2)
    finish(3)
    diagonal(0)
    diagonal(1)
    for copy in locals_[2:4]:
        copy.wait()
    in_place = order[0] == 0
    for s in range(S):
        col_ref[s] = jnp.where(in_place, m[s, pl.ds(0, N), :], m[1 - s, pl.ds(0, N), :])
        for h in range(2):
            row_ref[s, pl.ds(h * H, H), :] = jnp.where(in_place, rows[2 * s + h], rows[2 - 2 * s + h])
    totals = [add_diagonal(s) for s in range(S)]
    for s in range(S):
        total = jnp.where(in_place, totals[s], totals[1 - s])
        for h in range(2):
            chosen = jnp.where(in_place, dinv[s, pl.ds(h * H, H)], dinv[1 - s, pl.ds(h * H, H)])
            diag_ref[s, pl.ds(h * H, H), :] = chosen - total[:, h * N : (h + 1) * N]
    for copy in sent:
        copy.wait_send()
    for u in range(U):

        @pl.when(off_diagonal)
        def _(u=u):
            mirror(u).wait_send()


def on_device(resident_inverse, factor_panel, diag_inverse, ancestors, start_order):
    vmem = pl.BlockSpec(memory_space=pltpu.VMEM)
    hbm = pl.BlockSpec(memory_space=pltpu.HBM)
    dma = pltpu.SemaphoreType.DMA
    half = NZ // 2
    chips = len(CHIPS)
    row, col, diag = pl.pallas_call(
        kernel,
        out_shape=(
            jax.ShapeDtypeStruct((S, N, COLS), F32),
            jax.ShapeDtypeStruct((S, N, ROWS), F32),
            jax.ShapeDtypeStruct((S, N, N), F32),
        ),
        in_specs=[hbm] * 5,
        out_specs=(vmem, vmem, vmem),
        scratch_shapes=[
            pltpu.SMEM(start_order.shape, jnp.int32),
            pltpu.SMEM(ancestors.shape, jnp.int32),
            pltpu.VMEM((ROWS, COLS), F32),
            pltpu.VMEM((ROWS, COLS), BF),
            pltpu.VMEM((ROWS, COLS), BF),
            pltpu.VMEM((S, N, N), F32),
            pltpu.VMEM((U, NC, H, ROWS), F32),
            pltpu.VMEM((U, W, ROWS), BF),
            pltpu.VMEM((U, W, ROWS), BF),
            pltpu.VMEM((U, NZ, 2, H, COLS), F32),
            pltpu.VMEM((U, 2, 2, half - 1, H, COLS), F32),
            pltpu.VMEM((U, 2, 2, H, COLS), F32),
            pltpu.VMEM((U, H, COLS), F32),
            pltpu.VMEM((U, H, COLS), F32),
            pltpu.VMEM((S, 128, ROWS), F32),
            pltpu.VMEM((S, NR, 8, 128), F32),
            pltpu.VMEM((S, NR - 1, 8, 128), F32),
            dma((8,)),
            dma((U, chips)),
            dma((U, chips)),
            dma((U,)),
            dma((U,)),
            dma((U, chips)),
            dma((U, chips)),
            dma((U, 2, 2, half)),
            dma((U, 2, 2, half - 1)),
            dma((U, 2, 2)),
            dma((U,)),
            dma((U,)),
            dma((U,)),
            dma((U,)),
            dma((S, NR - 1)),
            dma((S, NR - 1)),
        ],
        compiler_params=pltpu.CompilerParams(
            collective_id=0, has_side_effects=True, vmem_limit_bytes=60 * 1024 * 1024
        ),
        name="selected_inverse",
    )(start_order, ancestors, resident_inverse, jnp.swapaxes(factor_panel, 1, 2), diag_inverse)
    return jnp.swapaxes(col, 1, 2), row, diag


def solution(mesh):
    return jax.shard_map(
        on_device,
        mesh=mesh,
        in_specs=(P("row", "col"), P(None, "row", "col"), P(None, "row", "col"), P(), P()),
        out_specs=(P(None, "row", "col"), P(None, "row", "col"), P(None, "row", "col")),
        check_vma=False,
    )
```

time: 149 us -> 62.5 us (0.42)
  blocking collectives: 77 us -> 0 us
  Pallas kernels: 0 us -> 57.2 us
  waiting for transfers between devices: 38.5 us -> 0 us
  starting transfers between devices: 15.1 us -> 0 us
  matrix products: 5.46 us -> 0 us
  other arithmetic: 5.27 us -> 0 us
  local copies, waits for them, and re-layouts: 6.22 us -> 4.4 us
    all_to_all x2 -> x0, blocking collectives: 77 us -> none  [the longest x1 47.4 us: sent_and_summed(): lax.all_to_all(pieces, axis, split_axis=0, concat_axis=0, tiled=True)]
    pallas_call x0 -> x1, Pallas kernels: none -> 57.2 us  [on_device(): pl.pallas_call(kernel, out_shape=(jax.ShapeDtypeStruct((S, N, COLS), F32)...]
    ppermute x8 -> x0, waiting for transfers between devices: 31.7 us -> none  [from_partner(): return lax.ppermute(block, axis, route)]
    ppermute x8 -> x0, starting transfers between devices: 10.1 us -> none  [from_partner(): return lax.ppermute(block, axis, route)]
    all_to_all x1 -> x0, waiting for transfers between devices: 6.83 us -> none  [sent_and_summed(): lax.all_to_all(pieces, axis, split_axis=0, concat_axis=0, tiled=True)]
    dot_general x2 -> x0, matrix products: 5.46 us -> none  [the longest x1 4.03 us: on_device(): jnp.einsum('sra,rc->sac', widened, resident_inverse, precision=lax.Precis...]
    all_to_all x1 -> x0, starting transfers between devices: 4.99 us -> none  [sent_and_summed(): lax.all_to_all(pieces, axis, split_axis=0, concat_axis=0, tiled=True)]
    unnamed x14 -> x3, local copies, waits for them, and re-layouts: 1.05 us -> 4.4 us
  transfers between devices with their start and end apart: 9 -> 0, of which waited for: 9 -> 0; matrix products, arithmetic and copies ran while one was open for 2% -> 0% of each run, Pallas kernels for 0% -> 0%
where the time goes in v2:
time: 62.5 us; the launch traced here: 62.3 us
  Pallas kernels  57.2 us (92%)
  local copies, waits for them, and re-layouts  4.4 us (7%)
  between operations  0.64 us (1%)
    pallas_call x1, Pallas kernels, on_device(): pl.pallas_call(kernel, out_shape=(jax.ShapeDtypeStruct((S, N, COLS), F32)...  57.2 us
    unnamed x3, local copies, waits for them, and re-layouts  4.4 us

profile of v2, /device:TPU:2, one launch (start us, length us, event | category | flops | bytes accessed | tf_op | source)
XLA Modules:
  0.0 62.3 jit_solution(15187104737914874039)
XLA Ops:
  0.6 57.2 %selected_inverse.1 = (f32[2,16,768]{2,1,0:T(8,128)}, f32[2,16,768]{2,1,0:T(8,128)}, f32[2,16,16]{2,1,0:T(8,128)}) custom-call(s32[2]{0:T(128)} %order_hbm.1, s32[2,48]{1,0:T(2,128)} %anc_hbm.1, f32[768,768]{1,0:T(8,128)} %a_hbm.1, f32[2,16,768]{2,1,0:T(8,128)} %bitcast.2, f32[2,16,16]{2,1,0:T(8,128)} %dinv_hbm.1), custom_call_target="tpu_custom_call" | custom-call | tf_op jit(solution)/shard_map/selected_inverse/pallas_call | solution.py:270
  57.9 1.5 %copy.11 = f32[2,768,16]{1,2,0:T(8,128)} copy(f32[2,768,16]{1,2,0:T(8,128)} %bitcast.3) | data formatting | bytes 196608
  59.4 1.5 %copy.12 = f32[2,16,768]{2,1,0:T(8,128)} copy(f32[2,16,768]{2,1,0:T(8,128)} %get-tuple-element.13) | data formatting | bytes 196608
  60.9 1.3 %copy.13 = f32[2,16,16]{2,1,0:T(8,128)} copy(f32[2,16,16]{2,1,0:T(8,128)} %get-tuple-element.14) | data formatting | bytes 4096

commit v3 on v2

--- a/solution.py
+++ b/solution.py
@@ -39,8 +39,8 @@
 def kernel(
     order_hbm, anc_hbm, a_hbm, p_hbm, dinv_hbm,
     row_ref, col_ref, diag_ref,
-    order, anc, a_buf, a_hi, a_lo, dinv, pt, p_hi, p_lo, t, rp, fin, xr, rows, m, dp, dr,
-    local_sem, ag_send, ag_recv, sib_send, sib_recv, fw_send, fw_recv,
+    order, anc, a_buf, a_hi, a_lo, dinv, outs, diags, pt, p_hi, p_lo, t, rp, fin, xr, rows, m, dp, dr,
+    local_sem, out_sem, ag_send, ag_recv, sib_send, sib_recv, fw_send,
     rs_send, rs_recv, fin_recv, x_send, x_recv, m_send, m_recv, d_send, d_recv,
 ):
     r = lax.axis_index("row")
@@ -88,6 +88,11 @@
         copy.start()
         sent.append(copy)
 
+    def settle():
+        for copy in sent:
+            copy.wait_send()
+        sent.clear()
+
     def spread(u):
         mine = p_hbm.at[u // 2, pl.ds(u % 2 * H, H)]
         for i, (dy, dx) in enumerate(CHIPS):
@@ -98,15 +103,12 @@
         for i, (dy, dx) in list(enumerate(CHIPS))[::-1]:
             slot = col_at(-dy, dx, k)
             remote(pt.at[u, slot], pt.at[u, slot], ag_send.at[u, i], ag_recv.at[u, i], sibling).wait_recv()
-            send(pt.at[u, slot], pt.at[u, slot], fw_send.at[u, i], fw_recv.at[u, i], sibling)
+            send(pt.at[u, slot], pt.at[u, slot], fw_send.at[u, i], sib_recv.at[u], sibling)
 
     def multiply(u):
         locals_[4 + u].wait()
-        other = col_at(0, 0, 1 - k)
-        remote(pt.at[u, other], pt.at[u, other], sib_send.at[u], sib_recv.at[u], sibling).wait_recv()
-        for i, (dy, dx) in enumerate(CHIPS):
-            slot = col_at(-dy, dx, 1 - k)
-            remote(pt.at[u, slot], pt.at[u, slot], fw_send.at[u, i], fw_recv.at[u, i], sibling).wait_recv()
+        half = pt.at[u, pl.ds(0, NC // 2)]
+        remote(half, half, sib_send.at[u], sib_recv.at[u], sibling).wait_recv()
         for b in range(TILES):
             here = pl.ds(b * TILE, TILE)
             flag = anc[u // 2, r * TILES + b].astype(F32)
@@ -188,12 +190,12 @@
         dp[s] = (halves[0] + pltpu.roll(halves[1], N, 1)).reshape(NR, 8, 128)
         for i, (dz, dx) in enumerate(ROW_PEERS):
             to = row_at(dz, dx)
-            send(dp.at[s, to], dr.at[s, i], d_send.at[s, i], d_recv.at[s, i], (to, c))
+            send(dp.at[s, to], dr.at[s, i], d_send.at[s, i], d_recv.at[s], (to, c))
 
     def add_diagonal(s):
         total = dp[s, r]
-        for i in list(range(NR - 1))[::-1]:
-            remote(dr.at[s, i], dr.at[s, i], d_send.at[s, i], d_recv.at[s, i], x_peer).wait_recv()
+        remote(dr.at[s], dr.at[s], d_send.at[s, 0], d_recv.at[s], x_peer).wait_recv()
+        for i in range(NR - 1):
             total += dr[s, i]
         return total
 
@@ -237,32 +239,58 @@
     hop(3, 3)
     finish(2)
     finish(3)
+    settle()
     diagonal(0)
     diagonal(1)
+    for u in range(U):
+
+        @pl.when(off_diagonal)
+        def _(u=u):
+            mirror(u).wait_send()
+
     for copy in locals_[2:4]:
         copy.wait()
     in_place = order[0] == 0
     for s in range(S):
-        col_ref[s] = jnp.where(in_place, m[s, pl.ds(0, N), :], m[1 - s, pl.ds(0, N), :])
+        outs[0, s] = jnp.where(in_place, m[s, pl.ds(0, N), :], m[1 - s, pl.ds(0, N), :])
         for h in range(2):
-            row_ref[s, pl.ds(h * H, H), :] = jnp.where(in_place, rows[2 * s + h], rows[2 - 2 * s + h])
+            outs[1, s, pl.ds(h * H, H), :] = jnp.where(in_place, rows[2 * s + h], rows[2 - 2 * s + h])
+    stores = [
+        pltpu.make_async_copy(outs.at[0], col_ref, out_sem.at[0]),
+        pltpu.make_async_copy(outs.at[1], row_ref, out_sem.at[1]),
+        pltpu.make_async_copy(diags, diag_ref, out_sem.at[2]),
+    ]
+    stores[0].start()
+    stores[1].start()
+    settle()
     totals = [add_diagonal(s) for s in range(S)]
     for s in range(S):
         total = jnp.where(in_place, totals[s], totals[1 - s])
         for h in range(2):
             chosen = jnp.where(in_place, dinv[s, pl.ds(h * H, H)], dinv[1 - s, pl.ds(h * H, H)])
-            diag_ref[s, pl.ds(h * H, H), :] = chosen - total[:, h * N : (h + 1) * N]
-    for copy in sent:
-        copy.wait_send()
-    for u in range(U):
-
-        @pl.when(off_diagonal)
-        def _(u=u):
-            mirror(u).wait_send()
+            diags[s, pl.ds(h * H, H), :] = chosen - total[:, h * N : (h + 1) * N]
+    stores[2].start()
+    for copy in stores:
+        copy.wait()
+
+
+def copy_out(*refs):
+    for i in range(3):
+        refs[3 + i][...] = refs[i][...]
+
+
+def deliver(*arrays):
+    return pl.pallas_call(
+        copy_out,
+        out_shape=tuple(jax.ShapeDtypeStruct(x.shape, x.dtype) for x in arrays),
+        in_specs=[pl.BlockSpec(memory_space=pltpu.VMEM)] * 3,
+        out_specs=(pl.BlockSpec(memory_space=pltpu.VMEM),) * 3,
+        scratch_shapes=[pltpu.VMEM(x.shape, x.dtype) for x in arrays] + [pltpu.SemaphoreType.DMA((6,))],
+        name="deliver",
+    )(*arrays)
 
 
 def on_device(resident_inverse, factor_panel, diag_inverse, ancestors, start_order):
-    vmem = pl.BlockSpec(memory_space=pltpu.VMEM)
     hbm = pl.BlockSpec(memory_space=pltpu.HBM)
     dma = pltpu.SemaphoreType.DMA
     half = NZ // 2
@@ -275,13 +303,15 @@
             jax.ShapeDtypeStruct((S, N, N), F32),
         ),
         in_specs=[hbm] * 5,
-        out_specs=(vmem, vmem, vmem),
+        out_specs=(hbm, hbm, hbm),
         scratch_shapes=[
             pltpu.SMEM(start_order.shape, jnp.int32),
             pltpu.SMEM(ancestors.shape, jnp.int32),
             pltpu.VMEM((ROWS, COLS), F32),
             pltpu.VMEM((ROWS, COLS), BF),
             pltpu.VMEM((ROWS, COLS), BF),
+            pltpu.VMEM((S, N, N), F32),
+            pltpu.VMEM((2, S, N, COLS), F32),
             pltpu.VMEM((S, N, N), F32),
             pltpu.VMEM((U, NC, H, ROWS), F32),
             pltpu.VMEM((U, W, ROWS), BF),
@@ -295,11 +325,11 @@
             pltpu.VMEM((S, NR, 8, 128), F32),
             pltpu.VMEM((S, NR - 1, 8, 128), F32),
             dma((8,)),
+            dma((3,)),
             dma((U, chips)),
             dma((U, chips)),
             dma((U,)),
             dma((U,)),
-            dma((U, chips)),
             dma((U, chips)),
             dma((U, 2, 2, half)),
             dma((U, 2, 2, half - 1)),
@@ -309,13 +339,14 @@
             dma((U,)),
             dma((U,)),
             dma((S, NR - 1)),
-            dma((S, NR - 1)),
+            dma((S,)),
         ],
         compiler_params=pltpu.CompilerParams(
             collective_id=0, has_side_effects=True, vmem_limit_bytes=60 * 1024 * 1024
         ),
         name="selected_inverse",
     )(start_order, ancestors, resident_inverse, jnp.swapaxes(factor_panel, 1, 2), diag_inverse)
+    row, col, diag = deliver(row, col, diag)
     return jnp.swapaxes(col, 1, 2), row, diag
 
 

time: 62.5 us -> 58.9 us (0.942)
  local copies, waits for them, and re-layouts: 4.4 us -> 0 us
  Pallas kernels: 57.2 us -> 58.1 us
    unnamed x3 -> x0, local copies, waits for them, and re-layouts: 4.4 us -> none
    pallas_call x0 -> x1, Pallas kernels: none -> 1.68 us  [deliver(): pl.pallas_call(copy_out, out_shape=tuple((jax.ShapeDtypeStruct(x.shape, x...]
    pallas_call x1, Pallas kernels: 57.2 us -> 56.4 us  [on_device(): pl.pallas_call(kernel, out_shape=(jax.ShapeDtypeStruct((S, N, COLS), F32)...]
where the time goes in v3:
time: 58.9 us; the launch traced here: 58.7 us
  Pallas kernels  58.1 us (99%)
  between operations  0.64 us (1%)
    pallas_call x1, Pallas kernels, on_device(): pl.pallas_call(kernel, out_shape=(jax.ShapeDtypeStruct((S, N, COLS), F32)...  56.4 us
    pallas_call x1, Pallas kernels, deliver(): pl.pallas_call(copy_out, out_shape=tuple((jax.ShapeDtypeStruct(x.shape, x...  1.68 us

profile of v3, /device:TPU:2, one launch (start us, length us, event | category | flops | bytes accessed | tf_op | source)
XLA Modules:
  0.0 58.7 jit_solution(11293675098597053643)
XLA Ops:
  0.6 56.4 %selected_inverse.1 = (f32[2,16,768]{2,1,0:T(8,128)}, f32[2,16,768]{2,1,0:T(8,128)}, f32[2,16,16]{2,1,0:T(8,128)}) custom-call(s32[2]{0:T(128)} %order_hbm.1, s32[2,48]{1,0:T(2,128)} %anc_hbm.1, f32[768,768]{1,0:T(8,128)} %a_hbm.1, f32[2,16,768]{2,1,0:T(8,128)} %bitcast.2, f32[2,16,16]{2,1,0:T(8,128)} %dinv_hbm.1), custom_call_target="tpu_custom_call" | custom-call | tf_op jit(solution)/shard_map/selected_inverse/pallas_call | solution.py:298
  57.0 1.7 %deliver.1 = (f32[2,16,768]{2,1,0:T(8,128)}, f32[2,16,768]{2,1,0:T(8,128)}, f32[2,16,16]{2,1,0:T(8,128)}) custom-call(f32[2,16,768]{2,1,0:T(8,128)} %get-tuple-element.9.refs_0_, f32[2,16,768]{2,1,0:T(8,128)} %get-tuple-element.10.refs_1_, f32[2,16,16]{2,1,0:T(8,128)} %get-tuple-element.11.refs_2_), custom_call_target="tpu_custom_call" | custom-call | tf_op jit(solution)/shard_map/deliver/pallas_call | solution.py:283

commit v4 on v3

v4 whole, which is shorter than its diff:
```python
import jax
import jax.numpy as jnp
from jax import lax
from jax.experimental import pallas as pl
from jax.experimental.pallas import tpu as pltpu
from jax.sharding import PartitionSpec as P

MESH = pl.DeviceIdType.MESH
BF = jnp.bfloat16
F32 = jnp.float32
TILE = 256
S = 2
U = 4
NR = 16
NC = 16
NZ = 8
NY = 4
ROWS = 768
COLS = 768
TILES = ROWS // TILE
N = 16
H = 8
V = NC // 2
W = V * H
CHIPS = [(2, 1), (1, 1), (3, 1), (2, 0), (0, 1), (1, 0), (3, 0)]
CHAINS = [(1, 0), (-1, 1), (-1, 0), (1, 1)]
ROW_PEERS = sorted(((j // 2, j % 2) for j in range(1, NR)), key=lambda p: -min(p[0], NZ - p[0]) - p[1])


def split(x):
    hi = x.astype(BF)
    lo = (x - hi.astype(F32)).astype(BF)
    return hi, lo


def hops(d, g):
    return NZ // 2 if (d == 1) == (g == 0) else NZ // 2 - 1


def kernel(
    order_hbm, anc_hbm, a_hbm, p_hbm, dinv_hbm,
    row_ref, col_ref, diag_ref,
    order, anc, a_buf, a_hi, a_lo, dinv, outs, diags, pt, p_hi, p_lo, t, rp, fin, rows, m, dp, dr,
    local_sem, out_sem, a_send, a_recv, ag_send, ag_recv, fw_send, fw_recv,
    rs_send, rs_recv, fin_recv, x_send, x_recv, m_send, m_recv, d_send, d_recv,
):
    r = lax.axis_index("row")
    c = lax.axis_index("col")
    z, xl = r // 2, r % 2
    y, xh, k = c // 4, (c // 2) % 2, c % 2
    off_diagonal = r != c

    def chip_at(dy, dx):
        return ((y + dy) % NY) * 2 + (xh + dx) % 2

    def row_at(dz, dx):
        return ((z + dz) % NZ) * 2 + (xl + dx) % 2

    sibling = (r, c + 1 - 2 * k)
    barrier = pltpu.get_barrier_semaphore()
    greeted = [(r, chip_at(dy, dx) * 2 + k) for dy, dx in CHIPS]
    for dz, dx in ((1, 0), (1, 1), (-1, 0), (-1, 1), (0, 1)):
        greeted += [(row_at(dz, dx), c), (row_at(dz, dx), c + 1 - 2 * k)]
    greeted.append(sibling)
    for device in greeted:
        pl.semaphore_signal(barrier, inc=1, device_id=device, device_id_type=MESH)

    locals_ = [
        pltpu.make_async_copy(a_hbm, a_buf.at[k], local_sem.at[0]),
        pltpu.make_async_copy(anc_hbm, anc, local_sem.at[1]),
        pltpu.make_async_copy(order_hbm, order, local_sem.at[2]),
        pltpu.make_async_copy(dinv_hbm, dinv, local_sem.at[3]),
    ]
    for u in range(U):
        mine = p_hbm.at[u // 2, pl.ds(u % 2 * H, H)]
        locals_.append(pltpu.make_async_copy(mine, pt.at[u, k, c // 2], local_sem.at[4 + u]))
    for copy in locals_:
        copy.start()
    pl.semaphore_wait(barrier, len(greeted))

    sent = []

    def remote(src, dst, send, recv, device):
        return pltpu.make_async_remote_copy(
            src_ref=src, dst_ref=dst, send_sem=send, recv_sem=recv, device_id=device, device_id_type=MESH
        )

    def send(*args):
        copy = remote(*args)
        copy.start()
        sent.append(copy)

    def settle():
        for copy in sent:
            copy.wait_send()
        sent.clear()

    def spread(u):
        mine = p_hbm.at[u // 2, pl.ds(u % 2 * H, H)]
        for i, (dy, dx) in enumerate(CHIPS):
            there = (r, chip_at(dy, dx) * 2 + k)
            send(mine, pt.at[u, k, c // 2], ag_send.at[u, i], ag_recv.at[u, i], there)

    def mask_and_split(u, core):
        for b in range(TILES):
            here = pl.ds(b * TILE, TILE)
            flag = anc[u // 2, r * TILES + b].astype(F32)
            hi, lo = split(pt[u, core, :, :, here].reshape(W, TILE) * flag)
            p_hi[u, core, :, here] = hi
            p_lo[u, core, :, here] = lo

    def gather(u):
        locals_[4 + u].wait()
        for i, (dy, dx) in list(enumerate(CHIPS))[::-1]:
            there = pt.at[u, k, chip_at(-dy, dx)]
            remote(there, there, ag_send.at[u, i], ag_recv.at[u, i], sibling).wait_recv()
        send(pt.at[u, k], pt.at[u, k], fw_send.at[u], fw_recv.at[u], sibling)
        mask_and_split(u, k)

    def multiply(u, core):
        for b in range(TILES):
            here = pl.ds(b * TILE, TILE)
            v, w = a_hi[core, :, here], a_lo[core, :, here]
            total = jnp.dot(p_hi[u, k], v, preferred_element_type=F32)
            total += jnp.dot(p_hi[u, k], w, preferred_element_type=F32)
            total += jnp.dot(p_lo[u, k], v, preferred_element_type=F32)
            t[u, core, :, :, here] = total.reshape(NZ, H, TILE)

    def other_half(u):
        there = pt.at[u, 1 - k]
        remote(there, there, fw_send.at[u], fw_recv.at[u], sibling).wait_recv()
        mask_and_split(u, 1 - k)

    def side(d):
        return 0 if d == 1 else 1

    def stay(core):
        return jnp.logical_and(xl == k, core == k)

    def own(u, core):
        there = (z * 2 + k, c - k + core)
        return remote(t.at[u, core, z], fin.at[u, 4 + xl], x_send.at[u, core], x_recv.at[u, xl], there)

    def hop(u, j):
        for d, core in CHAINS:
            last = hops(d, core) - 1
            if j > last:
                continue
            e = side(d)
            block = t.at[u, core, (z + d * (last + 1 - j)) % NZ]
            if j == 0:
                src = block
            else:
                src = rp.at[u, e, core, j - 1]
                remote(src, src, rs_send.at[u, e, core, j - 1], rs_recv.at[u, e, core, j - 1], sibling).wait_recv()
                src[...] += block[...]
            if j == last:
                there = (((z + d) % NZ) * 2 + k, c - k + core)
                send(src, fin.at[u, 2 * e + xl], rs_send.at[u, e, core, j], fin_recv.at[u], there)
            else:
                there = (row_at(d, 0), c)
                send(src, rp.at[u, e, core, j], rs_send.at[u, e, core, j], rs_recv.at[u, e, core, j], there)
        if j == 0:
            for core in range(2):

                @pl.when(stay(core))
                def _():
                    fin[u, 4 + xl] = t[u, core, z]

                @pl.when(jnp.logical_not(stay(core)))
                def _():
                    own(u, core).start()

    def mirror(u):
        there = m.at[u // 2, pl.ds(u % 2 * H, H)]
        return remote(rows.at[u], there, m_send.at[u], m_recv.at[u], (c, r))

    def finish(u):
        for x in range(2):

            @pl.when(jnp.logical_not(jnp.logical_and(xl == k, xl == x)))
            def _():
                there = fin.at[u, 4 + x]
                remote(there, there, x_send.at[u, 0], x_recv.at[u, x], sibling).wait_recv()

        there = fin.at[u, pl.ds(0, 4)]
        remote(there, there, rs_send.at[u, 0, 0, 0], fin_recv.at[u], sibling).wait_recv()
        for b in range(TILES):
            here = pl.ds(b * TILE, TILE)
            total = fin[u, 4, :, here] + fin[u, 5, :, here]
            total += fin[u, 0, :, here] + fin[u, 1, :, here]
            total += fin[u, 2, :, here] + fin[u, 3, :, here]
            rows[u, :, here] = total * -anc[u // 2, c * TILES + b].astype(F32)

        @pl.when(off_diagonal)
        def _():
            mirror(u).start()

        @pl.when(jnp.logical_not(off_diagonal))
        def _():
            m[u // 2, pl.ds(u % 2 * H, H), :] = rows[u]

    def diagonal(s):
        for h in range(2):

            @pl.when(off_diagonal)
            def _():
                mirror(2 * s + h).wait_recv()

        v, w = split(m[s])
        halves = []
        for h in range(2):
            total = jnp.zeros((2 * W, 128), F32)
            for left, right in ((p_hi, v), (p_hi, w), (p_lo, v)):
                panel = left[2 * s + h].reshape(2 * W, ROWS)
                total += lax.dot_general(panel, right, (((1,), (1,)), ((), ())), preferred_element_type=F32)
            halves.append(total)
        dp[s] = (halves[0] + pltpu.roll(halves[1], N, 1)).reshape(2, NZ, 8, 128)
        for i, (dz, dx) in enumerate(ROW_PEERS):
            part = dp.at[s, (xl + dx) % 2, (z + dz) % NZ]
            send(part, dr.at[s, i], d_send.at[s, i], d_recv.at[s], (row_at(dz, dx), c))

    def add_diagonal(s):
        total = dp[s, xl, z]
        remote(dr.at[s], dr.at[s], d_send.at[s, 0], d_recv.at[s], sibling).wait_recv()
        for i in range(NR - 1):
            total += dr[s, i]
        return total

    def split_inverse(core):
        for b in range(TILES):
            here = pl.ds(b * TILE, TILE)
            hi, lo = split(a_buf[core, here, :])
            a_hi[core, here, :] = hi
            a_lo[core, here, :] = lo

    spread(0)
    spread(1)
    spread(2)
    spread(3)
    send(a_hbm, a_buf.at[k], a_send, a_recv, sibling)
    m[:, pl.ds(N, 128 - N), :] = jnp.zeros((S, 128 - N, ROWS), F32)
    locals_[0].wait()
    split_inverse(k)
    locals_[1].wait()
    remote(a_hbm, a_buf.at[1 - k], a_send, a_recv, sibling).wait_recv()
    split_inverse(1 - k)
    gather(0)
    multiply(0, 0)
    multiply(0, 1)
    hop(0, 0)
    gather(1)
    multiply(1, 0)
    multiply(1, 1)
    hop(1, 0)
    gather(2)
    multiply(2, 0)
    multiply(2, 1)
    hop(0, 1)
    hop(2, 0)
    gather(3)
    multiply(3, 0)
    multiply(3, 1)
    hop(1, 1)
    hop(3, 0)
    other_half(0)
    hop(0, 2)
    hop(2, 1)
    other_half(1)
    hop(1, 2)
    hop(3, 1)
    hop(0, 3)
    other_half(2)
    hop(2, 2)
    hop(1, 3)
    other_half(3)
    hop(3, 2)
    finish(0)
    hop(2, 3)
    finish(1)
    hop(3, 3)
    finish(2)
    finish(3)
    for u in range(U):
        for core in range(2):

            @pl.when(jnp.logical_not(stay(core)))
            def _():
                own(u, core).wait_send()

    settle()
    diagonal(0)
    diagonal(1)
    for u in range(U):

        @pl.when(off_diagonal)
        def _(u=u):
            mirror(u).wait_send()

    for copy in locals_[2:4]:
        copy.wait()
    in_place = order[0] == 0
    for s in range(S):
        outs[0, s] = jnp.where(in_place, m[s, pl.ds(0, N), :], m[1 - s, pl.ds(0, N), :])
        for h in range(2):
            outs[1, s, pl.ds(h * H, H), :] = jnp.where(in_place, rows[2 * s + h], rows[2 - 2 * s + h])
    stores = [
        pltpu.make_async_copy(outs.at[0], col_ref, out_sem.at[0]),
        pltpu.make_async_copy(outs.at[1], row_ref, out_sem.at[1]),
        pltpu.make_async_copy(diags, diag_ref, out_sem.at[2]),
    ]
    stores[0].start()
    stores[1].start()
    settle()
    totals = [add_diagonal(s) for s in range(S)]
    for s in range(S):
        total = jnp.where(in_place, totals[s], totals[1 - s])
        for h in range(2):
            chosen = jnp.where(in_place, dinv[s, pl.ds(h * H, H)], dinv[1 - s, pl.ds(h * H, H)])
            diags[s, pl.ds(h * H, H), :] = chosen - total[:, h * N : (h + 1) * N]
    stores[2].start()
    for copy in stores:
        copy.wait()


def copy_out(*refs):
    for i in range(3):
        refs[3 + i][...] = refs[i][...]


def deliver(*arrays):
    return pl.pallas_call(
        copy_out,
        out_shape=tuple(jax.ShapeDtypeStruct(x.shape, x.dtype) for x in arrays),
        in_specs=[pl.BlockSpec(memory_space=pltpu.VMEM)] * 3,
        out_specs=(pl.BlockSpec(memory_space=pltpu.VMEM),) * 3,
        scratch_shapes=[pltpu.VMEM(x.shape, x.dtype) for x in arrays] + [pltpu.SemaphoreType.DMA((6,))],
        name="deliver",
    )(*arrays)


def on_device(resident_inverse, factor_panel, diag_inverse, ancestors, start_order):
    hbm = pl.BlockSpec(memory_space=pltpu.HBM)
    dma = pltpu.SemaphoreType.DMA
    half = NZ // 2
    chips = len(CHIPS)
    row, col, diag = pl.pallas_call(
        kernel,
        out_shape=(
            jax.ShapeDtypeStruct((S, N, COLS), F32),
            jax.ShapeDtypeStruct((S, N, ROWS), F32),
            jax.ShapeDtypeStruct((S, N, N), F32),
        ),
        in_specs=[hbm] * 5,
        out_specs=(hbm, hbm, hbm),
        scratch_shapes=[
            pltpu.SMEM(start_order.shape, jnp.int32),
            pltpu.SMEM(ancestors.shape, jnp.int32),
            pltpu.VMEM((2, ROWS, COLS), F32),
            pltpu.VMEM((2, ROWS, COLS), BF),
            pltpu.VMEM((2, ROWS, COLS), BF),
            pltpu.VMEM((S, N, N), F32),
            pltpu.VMEM((2, S, N, COLS), F32),
            pltpu.VMEM((S, N, N), F32),
            pltpu.VMEM((U, 2, V, H, ROWS), F32),
            pltpu.VMEM((U, 2, W, ROWS), BF),
            pltpu.VMEM((U, 2, W, ROWS), BF),
            pltpu.VMEM((U, 2, NZ, H, COLS), F32),
            pltpu.VMEM((U, 2, 2, half - 1, H, COLS), F32),
            pltpu.VMEM((U, 6, H, COLS), F32),
            pltpu.VMEM((U, H, COLS), F32),
            pltpu.VMEM((S, 128, ROWS), F32),
            pltpu.VMEM((S, 2, NZ, 8, 128), F32),
            pltpu.VMEM((S, NR - 1, 8, 128), F32),
            dma((8,)),
            dma((3,)),
            dma,
            dma,
            dma((U, chips)),
            dma((U, chips)),
            dma((U,)),
            dma((U,)),
            dma((U, 2, 2, half)),
            dma((U, 2, 2, half - 1)),
            dma((U,)),
            dma((U, 2)),
            dma((U, 2)),
            dma((U,)),
            dma((U,)),
            dma((S, NR - 1)),
            dma((S,)),
        ],
        compiler_params=pltpu.CompilerParams(
            collective_id=0, has_side_effects=True, vmem_limit_bytes=60 * 1024 * 1024
        ),
        name="selected_inverse",
    )(start_order, ancestors, resident_inverse, jnp.swapaxes(factor_panel, 1, 2), diag_inverse)
    row, col, diag = deliver(row, col, diag)
    return jnp.swapaxes(col, 1, 2), row, diag


def solution(mesh):
    return jax.shard_map(
        on_device,
        mesh=mesh,
        in_specs=(P("row", "col"), P(None, "row", "col"), P(None, "row", "col"), P(), P()),
        out_specs=(P(None, "row", "col"), P(None, "row", "col"), P(None, "row", "col")),
        check_vma=False,
    )
```

time: 58.9 us -> 57.6 us (0.978)
  Pallas kernels: 58.1 us -> 56.8 us
    pallas_call x1, Pallas kernels: 56.4 us -> 55.2 us  [on_device(): pl.pallas_call(kernel, out_shape=(jax.ShapeDtypeStruct((S, N, COLS), F32)...]
where the time goes in v4:
time: 57.6 us; the launch traced here: 57.5 us
  Pallas kernels  56.8 us (99%)
  between operations  0.64 us (1%)
    pallas_call x1, Pallas kernels, on_device(): pl.pallas_call(kernel, out_shape=(jax.ShapeDtypeStruct((S, N, COLS), F32)...  55.2 us
    pallas_call x1, Pallas kernels, deliver(): pl.pallas_call(copy_out, out_shape=tuple((jax.ShapeDtypeStruct(x.shape, x...  1.68 us

profile of v4, /device:TPU:2, one launch (start us, length us, event | category | flops | bytes accessed | tf_op | source)
XLA Modules:
  0.0 57.5 jit_solution(17594262017730899095)
XLA Ops:
  0.6 55.2 %selected_inverse.1 = (f32[2,16,768]{2,1,0:T(8,128)}, f32[2,16,768]{2,1,0:T(8,128)}, f32[2,16,16]{2,1,0:T(8,128)}) custom-call(s32[2]{0:T(128)} %order_hbm.1, s32[2,48]{1,0:T(2,128)} %anc_hbm.1, f32[768,768]{1,0:T(8,128)} %a_hbm.1, f32[2,16,768]{2,1,0:T(8,128)} %bitcast.2, f32[2,16,16]{2,1,0:T(8,128)} %dinv_hbm.1), custom_call_target="tpu_custom_call" | custom-call | tf_op jit(solution)/shard_map/selected_inverse/pallas_call | solution.py:347
  55.8 1.7 %deliver.1 = (f32[2,16,768]{2,1,0:T(8,128)}, f32[2,16,768]{2,1,0:T(8,128)}, f32[2,16,16]{2,1,0:T(8,128)}) custom-call(f32[2,16,768]{2,1,0:T(8,128)} %get-tuple-element.9.refs_0_, f32[2,16,768]{2,1,0:T(8,128)} %get-tuple-element.10.refs_1_, f32[2,16,16]{2,1,0:T(8,128)} %get-tuple-element.11.refs_2_), custom_call_target="tpu_custom_call" | custom-call | tf_op jit(solution)/shard_map/deliver/pallas_call | solution.py:332

commit v5 on v4

--- a/solution.py
+++ b/solution.py
@@ -192,6 +192,8 @@
             total += fin[u, 2, :, here] + fin[u, 3, :, here]
             rows[u, :, here] = total * -anc[u // 2, c * TILES + b].astype(F32)
 
+
+    def reflect(u):
         @pl.when(off_diagonal)
         def _():
             mirror(u).start()
@@ -276,11 +278,15 @@
     other_half(3)
     hop(3, 2)
     finish(0)
+    reflect(0)
     hop(2, 3)
     finish(1)
     hop(3, 3)
+    reflect(1)
     finish(2)
+    reflect(2)
     finish(3)
+    reflect(3)
     for u in range(U):
         for core in range(2):
 

time: 57.6 us -> 57.4 us (level)
  no operation moved by 1% of the time
where the time goes in v5:
time: 57.4 us; the launch traced here: 57.3 us
  Pallas kernels  56.6 us (99%)
  between operations  0.64 us (1%)
    pallas_call x1, Pallas kernels, on_device(): pl.pallas_call(kernel, out_shape=(jax.ShapeDtypeStruct((S, N, COLS), F32)...  55 us
    pallas_call x1, Pallas kernels, deliver(): pl.pallas_call(copy_out, out_shape=tuple((jax.ShapeDtypeStruct(x.shape, x...  1.68 us

profile of v5, /device:TPU:2, one launch (start us, length us, event | category | flops | bytes accessed | tf_op | source)
XLA Modules:
  0.0 57.3 jit_solution(5809851105488988718)
XLA Ops:
  0.6 55.0 %selected_inverse.1 = (f32[2,16,768]{2,1,0:T(8,128)}, f32[2,16,768]{2,1,0:T(8,128)}, f32[2,16,16]{2,1,0:T(8,128)}) custom-call(s32[2]{0:T(128)} %order_hbm.1, s32[2,48]{1,0:T(2,128)} %anc_hbm.1, f32[768,768]{1,0:T(8,128)} %a_hbm.1, f32[2,16,768]{2,1,0:T(8,128)} %bitcast.2, f32[2,16,16]{2,1,0:T(8,128)} %dinv_hbm.1), custom_call_target="tpu_custom_call" | custom-call | tf_op jit(solution)/shard_map/selected_inverse/pallas_call | solution.py:353
  55.6 1.7 %deliver.1 = (f32[2,16,768]{2,1,0:T(8,128)}, f32[2,16,768]{2,1,0:T(8,128)}, f32[2,16,16]{2,1,0:T(8,128)}) custom-call(f32[2,16,768]{2,1,0:T(8,128)} %get-tuple-element.9.refs_0_, f32[2,16,768]{2,1,0:T(8,128)} %get-tuple-element.10.refs_1_, f32[2,16,16]{2,1,0:T(8,128)} %get-tuple-element.11.refs_2_), custom_call_target="tpu_custom_call" | custom-call | tf_op jit(solution)/shard_map/deliver/pallas_call | solution.py:338

commit v6 on v5

--- a/solution.py
+++ b/solution.py
@@ -40,7 +40,7 @@
 def kernel(
     order_hbm, anc_hbm, a_hbm, p_hbm, dinv_hbm,
     row_ref, col_ref, diag_ref,
-    order, anc, a_buf, a_hi, a_lo, dinv, outs, diags, pt, p_hi, p_lo, t, rp, fin, rows, m, dp, dr,
+    order, anc, a_buf, a_hi, a_lo, dinv, outs, diags, pt, p, t, rp, fin, rows, m, dp, dr,
     local_sem, out_sem, a_send, a_recv, ag_send, ag_recv, fw_send, fw_recv,
     rs_send, rs_recv, fin_recv, x_send, x_recv, m_send, m_recv, d_send, d_recv,
 ):
@@ -106,8 +106,8 @@
             here = pl.ds(b * TILE, TILE)
             flag = anc[u // 2, r * TILES + b].astype(F32)
             hi, lo = split(pt[u, core, :, :, here].reshape(W, TILE) * flag)
-            p_hi[u, core, :, here] = hi
-            p_lo[u, core, :, here] = lo
+            p[u, core, 0, :, here] = hi
+            p[u, core, 1, :, here] = lo
 
     def gather(u):
         locals_[4 + u].wait()
@@ -121,9 +121,9 @@
         for b in range(TILES):
             here = pl.ds(b * TILE, TILE)
             v, w = a_hi[core, :, here], a_lo[core, :, here]
-            total = jnp.dot(p_hi[u, k], v, preferred_element_type=F32)
-            total += jnp.dot(p_hi[u, k], w, preferred_element_type=F32)
-            total += jnp.dot(p_lo[u, k], v, preferred_element_type=F32)
+            both = jnp.dot(p[u, k].reshape(2 * W, ROWS), v, preferred_element_type=F32)
+            total = jnp.dot(p[u, k, 0], w, preferred_element_type=F32)
+            total += both[:W] + both[W:]
             t[u, core, :, :, here] = total.reshape(NZ, H, TILE)
 
     def other_half(u):
@@ -213,8 +213,8 @@
         halves = []
         for h in range(2):
             total = jnp.zeros((2 * W, 128), F32)
-            for left, right in ((p_hi, v), (p_hi, w), (p_lo, v)):
-                panel = left[2 * s + h].reshape(2 * W, ROWS)
+            for left, right in ((0, v), (0, w), (1, v)):
+                panel = p[2 * s + h, :, left].reshape(2 * W, ROWS)
                 total += lax.dot_general(panel, right, (((1,), (1,)), ((), ())), preferred_element_type=F32)
             halves.append(total)
         dp[s] = (halves[0] + pltpu.roll(halves[1], N, 1)).reshape(2, NZ, 8, 128)
@@ -369,8 +369,7 @@
             pltpu.VMEM((2, S, N, COLS), F32),
             pltpu.VMEM((S, N, N), F32),
             pltpu.VMEM((U, 2, V, H, ROWS), F32),
-            pltpu.VMEM((U, 2, W, ROWS), BF),
-            pltpu.VMEM((U, 2, W, ROWS), BF),
+            pltpu.VMEM((U, 2, 2, W, ROWS), BF),
             pltpu.VMEM((U, 2, NZ, H, COLS), F32),
             pltpu.VMEM((U, 2, 2, half - 1, H, COLS), F32),
             pltpu.VMEM((U, 6, H, COLS), F32),

time: 57.4 us -> 56.9 us (level)
  no operation moved by 1% of the time
where the time goes in v6:
time: 56.9 us; the launch traced here: 56.8 us
  Pallas kernels  56.2 us (99%)
  between operations  0.64 us (1%)
    pallas_call x1, Pallas kernels, on_device(): pl.pallas_call(kernel, out_shape=(jax.ShapeDtypeStruct((S, N, COLS), F32)...  54.5 us
    pallas_call x1, Pallas kernels, deliver(): pl.pallas_call(copy_out, out_shape=tuple((jax.ShapeDtypeStruct(x.shape, x...  1.68 us

profile of v6, /device:TPU:2, one launch (start us, length us, event | category | flops | bytes accessed | tf_op | source)
XLA Modules:
  0.0 56.8 jit_solution(1823205974068921574)
XLA Ops:
  0.6 54.5 %selected_inverse.1 = (f32[2,16,768]{2,1,0:T(8,128)}, f32[2,16,768]{2,1,0:T(8,128)}, f32[2,16,16]{2,1,0:T(8,128)}) custom-call(s32[2]{0:T(128)} %order_hbm.1, s32[2,48]{1,0:T(2,128)} %anc_hbm.1, f32[768,768]{1,0:T(8,128)} %a_hbm.1, f32[2,16,768]{2,1,0:T(8,128)} %bitcast.2, f32[2,16,16]{2,1,0:T(8,128)} %dinv_hbm.1), custom_call_target="tpu_custom_call" | custom-call | tf_op jit(solution)/shard_map/selected_inverse/pallas_call | solution.py:353
  55.1 1.7 %deliver.1 = (f32[2,16,768]{2,1,0:T(8,128)}, f32[2,16,768]{2,1,0:T(8,128)}, f32[2,16,16]{2,1,0:T(8,128)}) custom-call(f32[2,16,768]{2,1,0:T(8,128)} %get-tuple-element.9.refs_0_, f32[2,16,768]{2,1,0:T(8,128)} %get-tuple-element.10.refs_1_, f32[2,16,16]{2,1,0:T(8,128)} %get-tuple-element.11.refs_2_), custom_call_target="tpu_custom_call" | custom-call | tf_op jit(solution)/shard_map/deliver/pallas_call | solution.py:338
